TPU v7x, 256 devices: a whole 4x4x8 slice. The times are simulated.
256 devices in a mesh: shot: 32 (over z, x_hi, core), dom: 8 (over y, x_lo).
Axes of the slice: x: 4 (x_hi: 2, x_lo: 2; x = x_hi * 2 + x_lo), y: 4, z: 8, core: 2. Of those that a mesh axis runs over, the one named last changes fastest.
Arguments:
- velocity: float32 [64, 128, 256], P('dom', 'shot'), may hold values from 0.15 to 0.4
- epsilon: float32 [64, 128, 256], P('dom', 'shot'), may hold values from 0.05 to 0.3
- forward_state: float32 [32, 4, 64, 128, 256], P('shot', None, 'dom'), may hold values from -1.2 to 1.2
- adjoint_state: float32 [32, 4, 64, 128, 256], P('shot', None, 'dom'), may hold values from -1.2 to 1.2
- source_cell: int32 [32], P('shot'), may hold values from 0 to 2097151
- wavelet: float32 [32, 3], P('shot'), may hold values from -6 to 6
- receiver_cells: int32 [32, 256], P('shot'), may hold values from 0 to 2097151
- residuals: float32 [32, 4, 256], P('shot'), may hold values from -6 to 6
Outputs:
- velocity_grad: float32 [64, 128, 256], P('dom', 'shot')
- epsilon_grad: float32 [64, 128, 256], P('dom', 'shot')
Inputs may be any that keep to these rules, and one draw needn't show every extreme that they name: `source_cell`: flat grid cell index (z * 128 + x) * 256 + y of each shot's source. `receiver_cells`: flat grid cell indices (z * 128 + x) * 256 + y of each shot's receivers; two receivers may share a cell.
All inputs are finite; a program needn't handle non-finite values.
Results may differ from a plain program's by a relative error of at most 0.00002.
Values sent between devices are 32-bit elements; how exact they have to be, the bound alone decides.
No kernel may reach another device: no remote copies, remote signals or barrier semaphores. Data moves between devices by JAX's collectives and lax.ppermute only.
A program may use at most 128 MiB of HBM per device.

v0:
```python
import jax
import jax.numpy as jnp
from jax import lax
from jax.sharding import PartitionSpec as P

STEPS = 4


def with_halo(cells, sides, width):
    for axis, dim in sides:
        count = lax.axis_size(axis)
        ends = count - 1
        head = lax.slice_in_dim(cells, 0, width, axis=dim)
        tail = lax.slice_in_dim(cells, cells.shape[dim] - width, cells.shape[dim], axis=dim)
        cells = jnp.concatenate(
            [
                lax.ppermute(tail, axis, [(i, (i + 1) % count) for i in range(ends)]),
                cells,
                lax.ppermute(head, axis, [((i + 1) % count, i) for i in range(ends)]),
            ],
            axis=dim,
        )
    return cells


def stencil(padded, axis, size):

    def part(offset):
        return lax.slice_in_dim(padded, offset, offset + size, axis=axis)

    return 4.0 / 3.0 * (part(1) + part(3)) - 1.0 / 12.0 * (part(0) + part(4)) - 2.5 * part(2)


def second_diff(field, axis):
    widths = [(0, 0), (0, 0), (0, 0)]
    widths[axis] = (2, 2)
    return stencil(jnp.pad(field, widths), axis, field.shape[axis])


def lateral(field):
    return second_diff(field, 1) + second_diff(field, 2)


def forward_vertical(field):
    padded = with_halo(field, (("dom", 0),), 2)
    return stencil(padded, 0, field.shape[0])


def adjoint_vertical(field):
    padded = with_halo(field, (("dom", 0),), 2)
    return stencil(padded, 0, field.shape[0])


def sum_shots(first_term, second_term, share_rows):
    whole_one, whole_two = lax.psum((first_term, second_term), "shot")
    offset = lax.axis_index("shot") * share_rows
    return (
        lax.dynamic_slice_in_dim(whole_one, offset, share_rows, 1),
        lax.dynamic_slice_in_dim(whole_two, offset, share_rows, 1),
    )


def on_device(
    velocity, epsilon, forward_state, adjoint_state, source_cell, wavelet, receiver_cells, residuals
):
    vel_slab, eps_slab = (
        lax.all_gather(velocity, "shot", axis=1, tiled=True),
        lax.all_gather(epsilon, "shot", axis=1, tiled=True),
    )
    stiffness = vel_slab * vel_slab
    stretch = 1.0 + 2.0 * eps_slab
    slab_depth, slab_width, slab_length = stiffness.shape
    plane_size = slab_width * slab_length
    first_layer = lax.axis_index("dom") * slab_depth

    def inject(field, cell_ids, amounts):
        layer_ids = cell_ids // plane_size - first_layer
        inside = (layer_ids >= 0) & (layer_ids < slab_depth)
        layer_ids = jnp.where(inside, layer_ids, 0)
        within = cell_ids % plane_size
        flattened = (
            field.reshape(-1)
            .at[layer_ids * plane_size + within]
            .add(jnp.where(inside, amounts, 0.0))
        )
        return flattened.reshape(field.shape)

    source = source_cell[0]
    receivers = receiver_cells[0]
    pressure_old, pressure_now = (forward_state[0, 0], forward_state[0, 1])
    support_old, support_now = (forward_state[0, 2], forward_state[0, 3])
    flat_terms = []
    depth_terms = []
    for moment in range(STEPS):
        flat_term = lateral(pressure_now)
        depth_term = forward_vertical(support_now)
        flat_terms.append(flat_term)
        depth_terms.append(depth_term)
        if moment + 1 < STEPS:
            pressure_new = (
                2.0 * pressure_now - pressure_old + stiffness * (stretch * flat_term + depth_term)
            )
            support_new = 2.0 * support_now - support_old + stiffness * (flat_term + depth_term)
            pressure_new = inject(pressure_new, source, wavelet[0, moment])
            support_new = inject(support_new, source, wavelet[0, moment])
            pressure_old, pressure_now = (pressure_now, pressure_new)
            support_old, support_now = (support_now, support_new)
    back_old, back_now = (adjoint_state[0, 0], adjoint_state[0, 1])
    side_old, side_now = (adjoint_state[0, 2], adjoint_state[0, 3])
    image_one = jnp.zeros_like(stiffness)
    image_two = jnp.zeros_like(stiffness)
    for moment in reversed(range(STEPS)):
        back_new = 2.0 * back_now - back_old + lateral(stiffness * (stretch * back_now + side_now))
        back_new = inject(back_new, receivers, residuals[0, moment])
        side_new = 2.0 * side_now - side_old + adjoint_vertical(stiffness * (back_now + side_now))
        image_one = image_one + back_new * flat_terms[moment]
        image_two = (
            image_two
            + back_new * depth_terms[moment]
            + side_new * (flat_terms[moment] + depth_terms[moment])
        )
        back_old, back_now = (back_now, back_new)
        side_old, side_now = (side_now, side_new)
    share_rows = velocity.shape[1]
    vel_term = 2.0 * vel_slab * (stretch * image_one + image_two)
    eps_term = 2.0 * stiffness * image_one
    velocity_grad, epsilon_grad = sum_shots(vel_term, eps_term, share_rows)
    return (velocity_grad, epsilon_grad)


def solution(mesh):
    placed = (
        P("dom", "shot", None),
        P("dom", "shot", None),
        P("shot", None, "dom", None, None),
        P("shot", None, "dom", None, None),
        P("shot"),
        P("shot", None),
        P("shot", None),
        P("shot", None, None),
    )
    return jax.shard_map(
        on_device,
        mesh=mesh,
        in_specs=placed,
        out_specs=(P("dom", "shot", None), P("dom", "shot", None)),
        check_vma=False,
    )
```

profile of v0, /device:TPU:1, one launch (start us, length us, event | category | flops | bytes accessed | tf_op | source)
XLA Modules:
  0.0 653.6 jit_solution(7060213678199251076)
XLA Ops:
  20.1 7.6 %collective-permute-done.1 = f32[2,128,256]{2,1,0:T(8,128)S(1)} collective-permute-done((f32[2,128,256]{2,1,0:T(8,128)S(1)}, f32[2,128,256]{2,1,0:T(8,128)S(1)}, u32[]{:S(2)}, u32[]{:S(2)}) %collective-permute-start.1) | collective-permute-done | bytes 262176 | tf_op jit(solution)/shard_map/ppermute | solution.py:19
  27.7 65.5 %all-gather.3.cloned.1.call-done = f32[8,128,256]{2,0,1:T(8,128)} async-done(((f32[8,4,256]{2,0,1:T(8,128)}), f32[8,128,256]{2,0,1:T(8,128)}) %all-gather.3.cloned.1.call-update) | async-done | bytes 1048592 | tf_op jit(solution)/shard_map/all_gather | solution.py:67
  93.2 78.1 %all-gather.5.cloned.1.call-done = f32[8,128,256]{2,0,1:T(8,128)} async-done(((f32[8,4,256]{2,0,1:T(8,128)}), f32[8,128,256]{2,0,1:T(8,128)}) %all-gather.5.cloned.1.call-update) | async-done | bytes 1048592 | tf_op jit(solution)/shard_map/all_gather | solution.py:68
  171.3 5.2 fusion.121
  189.9 6.9 %collective-permute-done.3 = f32[2,128,256]{2,1,0:T(8,128)S(1)} collective-permute-done((f32[2,128,256]{2,1,0:T(8,128)}, f32[2,128,256]{2,1,0:T(8,128)S(1)}, u32[]{:S(2)}, u32[]{:S(2)}) %collective-permute-start.3) | collective-permute-done | bytes 262176 | tf_op jit(solution)/shard_map/ppermute | solution.py:19
  196.8 4.2 multiply_add_fusion.4
  208.1 4.9 collective-permute-start.4
  227.7 4.4 collective-permute-done.5
  243.1 5.0 fusion.123
  256.7 4.2 scatter_fusion
  262.7 5.0 add_multiply_fusion.5
  267.8 4.0 add_multiply_fusion.4
  273.7 4.5 collective-permute-start.8
  288.8 4.3 scatter_fusion.1
  296.4 4.9 add_multiply_fusion.2
  302.2 4.6 collective-permute-start.10
  312.0 4.1 scatter_fusion.2
  318.7 6.1 add_multiply_fusion.1
  327.4 4.3 scatter_fusion.3
  334.3 9.8 %multiply_multiply_fusion = (f32[8,128,256]{2,1,0:T(8,128)}, f32[8,128,256]{2,1,0:T(8,128)}, f32[8,128,256]{2,1,0:T(8,128)}) fusion(f32[8,128,256]{2,1,0:T(8,128)} %reshape.380, f32[8,128,256]{2,1,0:T(8,128)} %copy-done.13, f32[8,128,256]{2,1,0:T(8,128)} %reshape.378, f32[8,128,256]{2,1,0:T(8,128)} %copy-done.15, f32[8,128,256]{2,1,0:T(8,128)S(1)} %reshape.376, ...), kind=kLoop, calls=%fused_computation.209 | loop fusion | flops 6815744 | bytes 13631488 | tf_op jit(solution)/shard_map/mul | solution.py:126
  345.3 4.9 collective-permute-start.14
  353.9 5.5 collective-permute-done.15
  359.5 7.9 %fusion.9 = f32[8,128,256]{2,1,0:T(8,128)} fusion(f32[8,128,256]{2,1,0:T(8,128)} %get-tuple-element.104, f32[2,128,256]{2,1,0:T(8,128)S(1)} %collective-permute-done.15, f32[2,128,256]{2,1,0:T(8,128)S(1)} %collective-permute-done.14, f32[8,128,256]{2,1,0:T(8,128)S(1)} %copy-done.11, f32[8,128,256]{2,1,0:T(8,128)} %get-tuple-element.92, ...), kind=kLoop, calls=%fused_computation.65 | loop fusion | flops 13893632 | bytes 24641536 | tf_op jit(solution)/shard_map/mul | solution.py:125
  367.4 277.9 %all-reduce.19.cloned.1.call-done = (f32[8,128,256]{2,1,0:T(8,128)}, f32[8,128,256]{2,1,0:T(8,128)}) async-done(((f32[8,128,256]{2,1,0:T(8,128)}, f32[8,128,256]{2,1,0:T(8,128)}), (f32[8,128,256]{2,1,0:T(8,128)}, f32[8,128,256]{2,1,0:T(8,128)})) %all-reduce.19.cloned.1.call-update) | async-done | bytes 2097168 | tf_op jit(solution)/shard_map/psum | solution.py:55
  (165 shorter events, 102.7 us)
Async XLA Ops:
  7.2 86.1 %all-gather.3.cloned.1.call-start = ((), (), s32[]{:S(2)}) async-start(), calls=%async_computation | async-start | bytes 1081344 | tf_op jit(solution)/shard_map/all_gather | solution.py:67
  8.6 162.7 %all-gather.5.cloned.1.call-start = ((), (), s32[]{:S(2)}) async-start(), calls=%async_computation.1 | async-start | bytes 1081344 | tf_op jit(solution)/shard_map/all_gather | solution.py:68
  10.1 635.2 %all-reduce.19.cloned.1.call-start = ((), (), s32[]{:S(2)}) async-start(), calls=%async_computation.2 | async-start | bytes 4194304 | tf_op jit(solution)/shard_map/psum | solution.py:55
  11.2 8.9 %collective-permute-start = (f32[2,128,256]{2,1,0:T(8,128)S(1)}, f32[2,128,256]{2,1,0:T(8,128)S(1)}, u32[]{:S(2)}, u32[]{:S(2)}) collective-permute-start(f32[2,128,256]{2,1,0:T(8,128)S(1)} %get-tuple-element.99), channel_id=1, source_target_pairs={{0,1},{1,2},{2,3},{3,4},{4,5},{5,6},{6,7},{8,9},{9,10},{10,11},{11... | collective-permute-start | bytes 786440 | tf_op jit(solution)/shard_map/ppermute | solution.py:17
  15.2 12.6 %collective-permute-start.1 = (f32[2,128,256]{2,1,0:T(8,128)S(1)}, f32[2,128,256]{2,1,0:T(8,128)S(1)}, u32[]{:S(2)}, u32[]{:S(2)}) collective-permute-start(f32[2,128,256]{2,1,0:T(8,128)S(1)} %get-tuple-element.100), channel_id=1, source_target_pairs={{1,0},{2,1},{3,2},{4,3},{5,4},{6,5},{7,6},{9,8},{10,9},{11,10},{12... | collective-permute-start | bytes 786440 | tf_op jit(solution)/shard_map/ppermute | solution.py:19
  27.7 143.6 %copy-start.31 = (f32[2,128,256]{2,1,0:T(8,128)}, f32[2,128,256]{2,1,0:T(8,128)S(1)}, u32[]{:S(2)}) copy-start(f32[2,128,256]{2,1,0:T(8,128)S(1)} %collective-permute-done.1) | copy-start | bytes 786436
  179.5 9.2 %collective-permute-start.2 = (f32[2,128,256]{2,1,0:T(8,128)}, f32[2,128,256]{2,1,0:T(8,128)}, u32[]{:S(2)}, u32[]{:S(2)}) collective-permute-start(f32[2,128,256]{2,1,0:T(8,128)} %slice.602), channel_id=1, source_target_pairs={{0,1},{1,2},{2,3},{3,4},{4,5},{5,6},{6,7},{8,9},{9,10},{10,11},{11... | collective-permute-start | bytes 786440 | tf_op jit(solution)/shard_map/ppermute | solution.py:17
  187.4 9.4 %collective-permute-start.3 = (f32[2,128,256]{2,1,0:T(8,128)}, f32[2,128,256]{2,1,0:T(8,128)S(1)}, u32[]{:S(2)}, u32[]{:S(2)}) collective-permute-start(f32[2,128,256]{2,1,0:T(8,128)} %slice.605), channel_id=1, source_target_pairs={{1,0},{2,1},{3,2},{4,3},{5,4},{6,5},{7,6},{9,8},{10,9},{11,10},{12... | collective-permute-start | bytes 786440 | tf_op jit(solution)/shard_map/ppermute | solution.py:19
  208.1 17.1 %collective-permute-start.4 = (f32[2,128,256]{2,1,0:T(8,128)}, f32[2,128,256]{2,1,0:T(8,128)}, u32[]{:S(2)}, u32[]{:S(2)}) collective-permute-start(f32[2,128,256]{2,1,0:T(8,128)} %slice.619), channel_id=1, source_target_pairs={{0,1},{1,2},{2,3},{3,4},{4,5},{5,6},{6,7},{8,9},{9,10},{10,11},{11... | collective-permute-start | bytes 786440 | tf_op jit(solution)/shard_map/ppermute | solution.py:17
  223.9 8.2 %collective-permute-start.5 = (f32[2,128,256]{2,1,0:T(8,128)}, f32[2,128,256]{2,1,0:T(8,128)S(1)}, u32[]{:S(2)}, u32[]{:S(2)}) collective-permute-start(f32[2,128,256]{2,1,0:T(8,128)} %slice.622), channel_id=1, source_target_pairs={{1,0},{2,1},{3,2},{4,3},{5,4},{6,5},{7,6},{9,8},{10,9},{11,10},{12... | collective-permute-start | bytes 786440 | tf_op jit(solution)/shard_map/ppermute | solution.py:19
  239.2 55.5 %collective-permute-start.12 = (f32[2,128,256]{2,1,0:T(8,128)}, f32[2,128,256]{2,1,0:T(8,128)}, u32[]{:S(2)}, u32[]{:S(2)}) collective-permute-start(f32[2,128,256]{2,1,0:T(8,128)} %slice.682), channel_id=1, source_target_pairs={{0,1},{1,2},{2,3},{3,4},{4,5},{5,6},{6,7},{8,9},{9,10},{10,11},{11... | collective-permute-start | bytes 786440 | tf_op jit(solution)/shard_map/ppermute | solution.py:17
  249.9 12.7 %collective-permute-start.6 = (f32[2,128,256]{2,1,0:T(8,128)}, f32[2,128,256]{2,1,0:T(8,128)}, u32[]{:S(2)}, u32[]{:S(2)}) collective-permute-start(f32[2,128,256]{2,1,0:T(8,128)} %get-tuple-element.125), channel_id=1, source_target_pairs={{0,1},{1,2},{2,3},{3,4},{4,5},{5,6},{6,7},{8,9},{9,10},{10,11},{11... | collective-permute-start | bytes 786440 | tf_op jit(solution)/shard_map/ppermute | solution.py:17
  252.7 10.1 %collective-permute-start.7 = (f32[2,128,256]{2,1,0:T(8,128)}, f32[2,128,256]{2,1,0:T(8,128)}, u32[]{:S(2)}, u32[]{:S(2)}) collective-permute-start(f32[2,128,256]{2,1,0:T(8,128)} %get-tuple-element.126), channel_id=1, source_target_pairs={{1,0},{2,1},{3,2},{4,3},{5,4},{6,5},{7,6},{9,8},{10,9},{11,10},{12... | collective-permute-start | bytes 786440 | tf_op jit(solution)/shard_map/ppermute | solution.py:19
  273.7 22.7 %collective-permute-start.8 = (f32[2,128,256]{2,1,0:T(8,128)}, f32[2,128,256]{2,1,0:T(8,128)}, u32[]{:S(2)}, u32[]{:S(2)}) collective-permute-start(f32[2,128,256]{2,1,0:T(8,128)} %get-tuple-element.121), channel_id=1, source_target_pairs={{0,1},{1,2},{2,3},{3,4},{4,5},{5,6},{6,7},{8,9},{9,10},{10,11},{11... | collective-permute-start | bytes 786440 | tf_op jit(solution)/shard_map/ppermute | solution.py:17
  278.2 18.2 %collective-permute-start.9 = (f32[2,128,256]{2,1,0:T(8,128)}, f32[2,128,256]{2,1,0:T(8,128)}, u32[]{:S(2)}, u32[]{:S(2)}) collective-permute-start(f32[2,128,256]{2,1,0:T(8,128)} %get-tuple-element.122), channel_id=1, source_target_pairs={{1,0},{2,1},{3,2},{4,3},{5,4},{6,5},{7,6},{9,8},{10,9},{11,10},{12... | collective-permute-start | bytes 786440 | tf_op jit(solution)/shard_map/ppermute | solution.py:19
  281.5 71.4 %collective-permute-start.13 = (f32[2,128,256]{2,1,0:T(8,128)}, f32[2,128,256]{2,1,0:T(8,128)}, u32[]{:S(2)}, u32[]{:S(2)}) collective-permute-start(f32[2,128,256]{2,1,0:T(8,128)} %slice.685), channel_id=1, source_target_pairs={{1,0},{2,1},{3,2},{4,3},{5,4},{6,5},{7,6},{9,8},{10,9},{11,10},{12... | collective-permute-start | bytes 786440 | tf_op jit(solution)/shard_map/ppermute | solution.py:19
  302.2 16.5 %collective-permute-start.10 = (f32[2,128,256]{2,1,0:T(8,128)}, f32[2,128,256]{2,1,0:T(8,128)S(1)}, u32[]{:S(2)}, u32[]{:S(2)}) collective-permute-start(f32[2,128,256]{2,1,0:T(8,128)} %get-tuple-element.119), channel_id=1, source_target_pairs={{0,1},{1,2},{2,3},{3,4},{4,5},{5,6},{6,7},{8,9},{9,10},{10,11},{11... | collective-permute-start | bytes 786440 | tf_op jit(solution)/shard_map/ppermute | solution.py:17
  306.8 11.9 %collective-permute-start.11 = (f32[2,128,256]{2,1,0:T(8,128)}, f32[2,128,256]{2,1,0:T(8,128)}, u32[]{:S(2)}, u32[]{:S(2)}) collective-permute-start(f32[2,128,256]{2,1,0:T(8,128)} %get-tuple-element.120), channel_id=1, source_target_pairs={{1,0},{2,1},{3,2},{4,3},{5,4},{6,5},{7,6},{9,8},{10,9},{11,10},{12... | collective-permute-start | bytes 786440 | tf_op jit(solution)/shard_map/ppermute | solution.py:19
  334.2 17.5 %copy-start.19 = (f32[8,128,256]{2,1,0:T(8,128)S(1)}, f32[8,128,256]{2,1,0:T(8,128)}, u32[]{:S(2)}) copy-start(f32[8,128,256]{2,1,0:T(8,128)} %reshape.382) | copy-start | bytes 3145732
  334.2 25.2 %copy-start.14 = (f32[8,128,256]{2,1,0:T(8,128)S(1)}, f32[8,128,256]{2,1,0:T(8,128)}, u32[]{:S(2)}) copy-start(f32[8,128,256]{2,1,0:T(8,128)} %copy-done.13) | copy-start | bytes 3145732
  334.3 25.2 %copy-start.16 = (f32[8,128,256]{2,1,0:T(8,128)S(1)}, f32[8,128,256]{2,1,0:T(8,128)}, u32[]{:S(2)}) copy-start(f32[8,128,256]{2,1,0:T(8,128)} %copy-done.15) | copy-start | bytes 3145732
  334.3 25.2 %copy-start.18 = (f32[8,128,256]{2,1,0:T(8,128)S(1)}, f32[8,128,256]{2,1,0:T(8,128)}, u32[]{:S(2)}) copy-start(f32[8,128,256]{2,1,0:T(8,128)} %get-tuple-element.81) | copy-start | bytes 3145732
  345.3 8.7 %collective-permute-start.14 = (f32[2,128,256]{2,1,0:T(8,128)S(1)}, f32[2,128,256]{2,1,0:T(8,128)S(1)}, u32[]{:S(2)}, u32[]{:S(2)}) collective-permute-start(f32[2,128,256]{2,1,0:T(8,128)S(1)} %get-tuple-element.117), channel_id=1, source_target_pairs={{0,1},{1,2},{2,3},{3,4},{4,5},{5,6},{6,7},{8,9},{9,10},{10,11},{11... | collective-permute-start | bytes 786440 | tf_op jit(solution)/shard_map/ppermute | solution.py:17
  350.2 9.2 %collective-permute-start.15 = (f32[2,128,256]{2,1,0:T(8,128)S(1)}, f32[2,128,256]{2,1,0:T(8,128)S(1)}, u32[]{:S(2)}, u32[]{:S(2)}) collective-permute-start(f32[2,128,256]{2,1,0:T(8,128)S(1)} %get-tuple-element.118), channel_id=1, source_target_pairs={{1,0},{2,1},{3,2},{4,3},{5,4},{6,5},{7,6},{9,8},{10,9},{11,10},{12... | collective-permute-start | bytes 786440 | tf_op jit(solution)/shard_map/ppermute | solution.py:19
  (30 other events, 166.6 us)
Sparse Core Ops, SparseCore 0:
  11.3 81.8 all-gather.2
  96.6 74.6 all-gather.4
  367.5 277.7 all-reduce.18
where the time goes:
time: 664 us; the launch traced here: 654 us
  waiting for transfers between devices  446 us (67%)
  other arithmetic  82.2 us (12%)
  local copies, waits for them, and re-layouts  65.1 us (10%)
  starting transfers between devices  43.1 us (6%)
  between operations  17.1 us (3%)
    psum x1, waiting for transfers between devices, sum_shots(): whole_one, whole_two = lax.psum((first_term, second_term), 'shot')  278 us
    all_gather x1, waiting for transfers between devices, on_device(): lax.all_gather(epsilon, 'shot', axis=1, tiled=True)  78.1 us
    all_gather x1, waiting for transfers between devices, on_device(): lax.all_gather(velocity, 'shot', axis=1, tiled=True)  65.5 us
    ppermute x8, starting transfers between devices, with_halo(): lax.ppermute(tail, axis, [(i, (i + 1) % count) for i in range(ends)])  32.4 us
    unnamed x85, local copies, waits for them, and re-layouts  26.9 us
    ppermute x8, waiting for transfers between devices, with_halo(): lax.ppermute(head, axis, [((i + 1) % count, i) for i in range(ends)])  24.6 us
    scatter-add x10, other arithmetic, inject(): flattened = field.reshape(-1).at[layer_ids * plane_size + within].add(jnp...  19.4 us
    reshape x10, local copies, waits for them, and re-layouts, inject(): return flattened.reshape(field.shape)  17.5 us
  transfers between devices with their start and end apart: 19, of which 8 were waited for; matrix products, arithmetic and copies ran while one was open for 16% of the time, Pallas kernels for 0%

commit v1 on v0

--- a/solution.py
+++ b/solution.py
@@ -4,6 +4,11 @@
 from jax.sharding import PartitionSpec as P
 
 STEPS = 4
+
+
+def gather_over(block, axis, dim):
+    sent = jnp.stack([block] * lax.axis_size(axis))
+    return jnp.concatenate(lax.all_to_all(sent, axis, 0, 0), axis=dim)
 
 
 def with_halo(cells, sides, width):
@@ -64,7 +69,7 @@
     velocity, epsilon, forward_state, adjoint_state, source_cell, wavelet, receiver_cells, residuals
 ):
     vel_slab, eps_slab = (
-        lax.all_gather(velocity, "shot", axis=1, tiled=True),
+        gather_over(velocity, "shot", 1),
         lax.all_gather(epsilon, "shot", axis=1, tiled=True),
     )
     stiffness = vel_slab * vel_slab

time: 664 us -> 637 us (0.959)
  waiting for transfers between devices: 446 us -> 348 us
  local copies, waits for them, and re-layouts: 65.1 us -> 101 us
  other arithmetic: 82.2 us -> 105 us
  starting transfers between devices: 43.1 us -> 56 us
    all_gather x1 -> x0, waiting for transfers between devices: 65.5 us -> none  [on_device(): lax.all_gather(velocity, 'shot', axis=1, tiled=True)]
    all_gather x1, waiting for transfers between devices: 78.1 us -> 52.8 us  [on_device(): lax.all_gather(epsilon, 'shot', axis=1, tiled=True)]
    ppermute x8, waiting for transfers between devices: 24.6 us -> 6.15 us  [with_halo(): lax.ppermute(head, axis, [((i + 1) % count, i) for i in range(ends)])]
    all_to_all x0 -> x1, starting transfers between devices: none -> 12.8 us  [gather_over(): return jnp.concatenate(lax.all_to_all(sent, axis, 0, 0), axis=dim)]
    reshape x10 -> x14, local copies, waits for them, and re-layouts: 17.5 us -> 29.8 us  [inject(): return flattened.reshape(field.shape)]
    all_to_all x0 -> x1, waiting for transfers between devices: none -> 9.13 us  [gather_over(): return jnp.concatenate(lax.all_to_all(sent, axis, 0, 0), axis=dim)]
    add x2, other arithmetic: 9.43 us -> 17.6 us  [on_device(): 2.0 * pressure_now - pressure_old]
    mul x3, other arithmetic: 12 us -> 19.5 us  [on_device(): stiffness * (stretch * back_now + side_now)]
  transfers between devices with their start and end apart: 19 -> 19, of which waited for: 8 -> 5; matrix products, arithmetic and copies ran while one was open for 16% -> 19% of each run, Pallas kernels for 0% -> 0%
where the time goes in v1:
time: 637 us; the launch traced here: 628 us
  waiting for transfers between devices  348 us (55%)
  other arithmetic  105 us (16%)
  local copies, waits for them, and re-layouts  101 us (16%)
  starting transfers between devices  56 us (9%)
  between operations  17.9 us (3%)
    psum x1, waiting for transfers between devices, sum_shots(): whole_one, whole_two = lax.psum((first_term, second_term), 'shot')  280 us
    all_gather x1, waiting for transfers between devices, on_device(): lax.all_gather(epsilon, 'shot', axis=1, tiled=True)  52.8 us
    ppermute x8, starting transfers between devices, with_halo(): lax.ppermute(tail, axis, [(i, (i + 1) % count) for i in range(ends)])  32.6 us
    reshape x14, local copies, waits for them, and re-layouts, inject(): return flattened.reshape(field.shape)  29.8 us
    unnamed x129, local copies, waits for them, and re-layouts  25.1 us
    scatter-add x10, other arithmetic, inject(): flattened = field.reshape(-1).at[layer_ids * plane_size + within].add(jnp...  24.8 us
    mul x3, other arithmetic, on_device(): stiffness * (stretch * back_now + side_now)  19.5 us
    add x2, other arithmetic, on_device(): 2.0 * pressure_now - pressure_old  17.6 us
  transfers between devices with their start and end apart: 19, of which 5 were waited for; matrix products, arithmetic and copies ran while one was open for 19% of the time, Pallas kernels for 0%

profile of v1, /device:TPU:1, one launch (start us, length us, event | category | flops | bytes accessed | tf_op | source)
XLA Modules:
  0.0 627.6 jit_solution(7487037487310886868)
XLA Ops:
  9.2 12.8 %all-to-all-start = ((f32[32,8,4,256]{3,2,1,0:T(4,128)}), f32[32,8,4,256]{3,2,1,0:T(4,128)}, u32[]{:S(2)}, u32[]{:S(2)}) async-start(f32[32,8,4,256]{3,2,1,0:T(4,128)} %stack.2), calls=%async_computation | async-start | bytes 2097152 | tf_op jit(solution)/shard_map/all_to_all | solution.py:11
  41.1 9.1 %all-to-all-done = f32[32,8,4,256]{3,2,1,0:T(4,128)} async-done(((f32[32,8,4,256]{3,2,1,0:T(4,128)}), f32[32,8,4,256]{3,2,1,0:T(4,128)}, u32[]{:S(2)}, u32[]{:S(2)}) %all-to-all-start) | async-done | bytes 1048608 | tf_op jit(solution)/shard_map/all_to_all | solution.py:11
  52.8 52.8 %all-gather.2.cloned.1.call-done = f32[8,128,256]{2,0,1:T(8,128)} async-done(((f32[8,4,256]{2,0,1:T(8,128)}), f32[8,128,256]{2,0,1:T(8,128)}) %all-gather.2.cloned.1.call-update) | async-done | bytes 1048592 | tf_op jit(solution)/shard_map/all_gather | solution.py:73
  105.6 11.3 %fusion.130 = (f32[8,128,256]{2,0,1:T(8,128)}, f32[8,128,256]{2,0,1:T(8,128)S(1)}, f32[8,128,256]{2,0,1:T(8,128)S(1)}) fusion(f32[1,1,8,128,256]{4,3,2,1,0:T(8,128)} %get-tuple-element.101, f32[32,8,4,256]{3,1,2,0:T(8,128)S(1)} %get-tuple-element.126, f32[8,128,256]{2,0,1:T(8,128)} %all-gather.2.cloned.1.call-done, ...), kind=kLoop, calls=%fused_computation.212 | loop fusion | flops 8650752 | bytes 9961472 | tf_op jit(solution)/shard_map/add | solution.py:106
  130.7 4.2 collective-permute-start.2
  146.8 6.3 %fusion.132 = (f32[8,128,256]{2,0,1:T(8,128)}, f32[8,128,256]{2,0,1:T(8,128)S(1)}, f32[8,128,256]{2,0,1:T(8,128)S(1)}) fusion(f32[32,8,4,256]{3,1,2,0:T(8,128)S(1)} %get-tuple-element.126, f32[8,128,256]{2,0,1:T(8,128)S(1)} %copy-done, f32[1,1,8,128,256]{4,3,2,1,0:T(8,128)S(1)} %get-tuple-element.102, f32[8,128,256]{2,1,0:T(8,128)S(1)} %copy-done.14, ...), kind=kLoop, calls=%fused_computation.233 | loop fusion | flops 8126464 | bytes 11796480 | tf_op jit(solution)/shard_map/add | solution.py:106
  166.9 4.4 collective-permute-start.4
  183.1 6.5 %fusion.135 = (f32[8,128,256]{2,0,1:T(8,128)}, f32[8,128,256]{2,0,1:T(8,128)S(1)}, f32[8,128,256]{2,0,1:T(8,128)S(1)}) fusion(f32[32,8,4,256]{3,1,2,0:T(8,128)S(1)} %get-tuple-element.126, f32[8,128,256]{2,1,0:T(8,128)S(1)} %copy-done.33, f32[8,128,256]{2,1,0:T(8,128)S(1)} %copy-done.18, f32[8,128,256]{2,0,1:T(8,128)S(1)} %copy.49, ...), kind=kLoop, calls=%fused_computation.236 | loop fusion | flops 7340032 | bytes 10747904 | tf_op jit(solution)/shard_map/add | solution.py:108
  194.4 4.0 collective-permute-start.6
  203.2 4.3 scatter_fusion
  209.6 6.5 %bitcast_multiply_fusion.7 = (f32[8,128,256]{2,0,1:T(8,128)S(1)}, f32[8,128,256]{2,0,1:T(8,128)S(1)}) fusion(f32[32,8,4,256]{3,1,2,0:T(8,128)S(1)} %get-tuple-element.126, f32[8,128,256]{2,1,0:T(8,128)S(1)} %reshape.367, f32[8,128,256]{2,0,1:T(8,128)S(1)} %copy-done, f32[8,128,256]{2,0,1:T(8,128)} %copy-done.41, f32[2,128,256]{2,0,1:T(2,128)} %collective-permute-done.7, ...), kind=kLoop, calls=%fused_computation.225 | loop fusion | flops 4980736 | bytes 8912896 | tf_op jit(solution)/shard_map/mul | solution.py:118
  220.8 4.0 collective-permute-start.8
  231.0 4.3 scatter_fusion.1
  237.8 6.2 bitcast_multiply_fusion.5
  248.9 4.7 collective-permute-start.10
  273.4 4.6 collective-permute-start.12
  281.1 4.4 scatter_fusion.2
  288.0 6.8 %bitcast_multiply_fusion.3 = (f32[8,128,256]{2,0,1:T(8,128)S(1)}, f32[8,128,256]{2,0,1:T(8,128)}) fusion(f32[32,8,4,256]{3,1,2,0:T(8,128)S(1)} %get-tuple-element.126, f32[8,128,256]{2,1,0:T(8,128)} %reshape.385, f32[8,128,256]{2,0,1:T(8,128)S(1)} %copy-done, f32[8,128,256]{2,0,1:T(8,128)} %copy-done.39, f32[2,128,256]{2,0,1:T(2,128)} %collective-permute-done.11, ...), kind=kLoop, calls=%fused_computation.221 | loop fusion | flops 4980736 | bytes 8912896 | tf_op jit(solution)/shard_map/mul | solution.py:118
  298.2 4.1 scatter_fusion.3
  304.9 12.3 %fusion.136 = (f32[8,128,256]{2,0,1:T(8,128)}, f32[8,128,256]{2,0,1:T(8,128)S(1)}, f32[8,128,256]{2,0,1:T(8,128)S(1)}) fusion(f32[32,8,4,256]{3,1,2,0:T(8,128)S(1)} %get-tuple-element.126, f32[8,128,256]{2,0,1:T(8,128)} %copy-done.10, f32[8,128,256]{2,1,0:T(8,128)} %reshape.387, f32[8,128,256]{2,0,1:T(8,128)} %copy-done.12, f32[8,128,256]{2,1,0:T(8,128)} %reshape.385, ...), kind=kLoop, calls=%fused_computation.237 | loop fusion | flops 6553600 | bytes 13631488 | tf_op jit(solution)/shard_map/mul | solution.py:131
  317.4 4.5 collective-permute-start.14
  325.3 5.6 collective-permute-done.15
  330.9 6.6 %fusion.69 = f32[8,128,256]{2,0,1:T(8,128)} fusion(f32[8,128,256]{2,0,1:T(8,128)S(1)} %get-tuple-element.112, f32[2,128,256]{2,0,1:T(2,128)S(1)} %collective-permute-done.15, f32[2,128,256]{2,0,1:T(2,128)S(1)} %collective-permute-done.14, f32[32,8,4,256]{3,1,2,0:T(8,128)S(1)} %copy-done.42, f32[8,128,256]{2,0,1:T(8,128)S(1)} %copy-done.9, ...), kind=kLoop, calls=%fused_computation.131 | loop fusion | flops 14155776 | bytes 22806528 | tf_op jit(solution)/shard_map/mul | solution.py:130
  337.6 279.9 %all-reduce.19.cloned.1.call-done = (f32[8,128,256]{2,0,1:T(8,128)}, f32[8,128,256]{2,0,1:T(8,128)}) async-done(((f32[8,128,256]{2,0,1:T(8,128)}, f32[8,128,256]{2,0,1:T(8,128)}), (f32[8,128,256]{2,0,1:T(8,128)}, f32[8,128,256]{2,0,1:T(8,128)})) %all-reduce.19.cloned.1.call-update) | async-done | bytes 2097168 | tf_op jit(solution)/shard_map/psum | solution.py:60
  (229 shorter events, 139.6 us)
Async XLA Ops:
  9.2 41.1 %all-to-all-start = ((f32[32,8,4,256]{3,2,1,0:T(4,128)}), f32[32,8,4,256]{3,2,1,0:T(4,128)}, u32[]{:S(2)}, u32[]{:S(2)}) async-start(f32[32,8,4,256]{3,2,1,0:T(4,128)} %stack.2), calls=%async_computation | async-start | bytes 2097152 | tf_op jit(solution)/shard_map/all_to_all | solution.py:11
  21.9 83.6 %all-gather.2.cloned.1.call-start = ((), (), s32[]{:S(2)}) async-start(), calls=%async_computation.1 | async-start | bytes 1081344 | tf_op jit(solution)/shard_map/all_gather | solution.py:73
  22.7 594.8 %all-reduce.19.cloned.1.call-start = ((), (), s32[]{:S(2)}) async-start(), calls=%async_computation.2 | async-start | bytes 4194304 | tf_op jit(solution)/shard_map/psum | solution.py:60
  24.7 28.1 %collective-permute-start = (f32[2,128,256]{2,0,1:T(2,128)}, f32[2,128,256]{2,0,1:T(2,128)S(1)}, u32[]{:S(2)}, u32[]{:S(2)}) collective-permute-start(f32[2,128,256]{2,0,1:T(2,128)} %bitcast.149), channel_id=1, source_target_pairs={{0,1},{1,2},{2,3},{3,4},{4,5},{5,6},{6,7},{8,9},{9,10},{10,11},{11... | collective-permute-start | bytes 786440 | tf_op jit(solution)/shard_map/ppermute | solution.py:22
  27.8 24.9 %collective-permute-start.1 = (f32[2,128,256]{2,0,1:T(2,128)}, f32[2,128,256]{2,0,1:T(2,128)}, u32[]{:S(2)}, u32[]{:S(2)}) collective-permute-start(f32[2,128,256]{2,0,1:T(2,128)} %bitcast.148), channel_id=1, source_target_pairs={{1,0},{2,1},{3,2},{4,3},{5,4},{6,5},{7,6},{9,8},{10,9},{11,10},{12... | collective-permute-start | bytes 786440 | tf_op jit(solution)/shard_map/ppermute | solution.py:24
  35.7 81.2 %copy-start.22 = (f32[1,1,8,128,256]{4,3,2,1,0:T(8,128)}, f32[1,1,8,128,256]{4,3,2,1,0:T(8,128)S(1)}, u32[]{:S(2)}) copy-start(f32[1,1,8,128,256]{4,3,2,1,0:T(8,128)S(1)} %get-tuple-element.100) | copy-start | bytes 3145732
  127.5 17.5 %collective-permute-start.3 = (f32[2,128,256]{2,0,1:T(2,128)}, f32[2,128,256]{2,0,1:T(2,128)}, u32[]{:S(2)}, u32[]{:S(2)}) collective-permute-start(f32[2,128,256]{2,0,1:T(2,128)} %copy.45), channel_id=1, source_target_pairs={{1,0},{2,1},{3,2},{4,3},{5,4},{6,5},{7,6},{9,8},{10,9},{11,10},{12... | collective-permute-start | bytes 786440 | tf_op jit(solution)/shard_map/ppermute | solution.py:24
  130.7 16.1 %collective-permute-start.2 = (f32[2,128,256]{2,0,1:T(2,128)}, f32[2,128,256]{2,0,1:T(2,128)S(1)}, u32[]{:S(2)}, u32[]{:S(2)}) collective-permute-start(f32[2,128,256]{2,0,1:T(2,128)} %copy.43), channel_id=1, source_target_pairs={{0,1},{1,2},{2,3},{3,4},{4,5},{5,6},{6,7},{8,9},{9,10},{10,11},{11... | collective-permute-start | bytes 786440 | tf_op jit(solution)/shard_map/ppermute | solution.py:22
  163.7 17.6 %collective-permute-start.5 = (f32[2,128,256]{2,0,1:T(2,128)}, f32[2,128,256]{2,0,1:T(2,128)}, u32[]{:S(2)}, u32[]{:S(2)}) collective-permute-start(f32[2,128,256]{2,0,1:T(2,128)} %copy.58), channel_id=1, source_target_pairs={{1,0},{2,1},{3,2},{4,3},{5,4},{6,5},{7,6},{9,8},{10,9},{11,10},{12... | collective-permute-start | bytes 786440 | tf_op jit(solution)/shard_map/ppermute | solution.py:24
  166.9 16.2 %collective-permute-start.4 = (f32[2,128,256]{2,0,1:T(2,128)}, f32[2,128,256]{2,0,1:T(2,128)S(1)}, u32[]{:S(2)}, u32[]{:S(2)}) collective-permute-start(f32[2,128,256]{2,0,1:T(2,128)} %copy.56), channel_id=1, source_target_pairs={{0,1},{1,2},{2,3},{3,4},{4,5},{5,6},{6,7},{8,9},{9,10},{10,11},{11... | collective-permute-start | bytes 786440 | tf_op jit(solution)/shard_map/ppermute | solution.py:22
  194.4 14.6 %collective-permute-start.6 = (f32[2,128,256]{2,0,1:T(2,128)}, f32[2,128,256]{2,0,1:T(2,128)S(1)}, u32[]{:S(2)}, u32[]{:S(2)}) collective-permute-start(f32[2,128,256]{2,0,1:T(2,128)} %get-tuple-element.137), channel_id=1, source_target_pairs={{0,1},{1,2},{2,3},{3,4},{4,5},{5,6},{6,7},{8,9},{9,10},{10,11},{11... | collective-permute-start | bytes 786440 | tf_op jit(solution)/shard_map/ppermute | solution.py:22
  198.4 11.2 %collective-permute-start.7 = (f32[2,128,256]{2,0,1:T(2,128)}, f32[2,128,256]{2,0,1:T(2,128)}, u32[]{:S(2)}, u32[]{:S(2)}) collective-permute-start(f32[2,128,256]{2,0,1:T(2,128)} %get-tuple-element.138), channel_id=1, source_target_pairs={{1,0},{2,1},{3,2},{4,3},{5,4},{6,5},{7,6},{9,8},{10,9},{11,10},{12... | collective-permute-start | bytes 786440 | tf_op jit(solution)/shard_map/ppermute | solution.py:24
  220.8 17.0 %collective-permute-start.8 = (f32[2,128,256]{2,0,1:T(2,128)}, f32[2,128,256]{2,0,1:T(2,128)S(1)}, u32[]{:S(2)}, u32[]{:S(2)}) collective-permute-start(f32[2,128,256]{2,0,1:T(2,128)} %get-tuple-element.133), channel_id=1, source_target_pairs={{0,1},{1,2},{2,3},{3,4},{4,5},{5,6},{6,7},{8,9},{9,10},{10,11},{11... | collective-permute-start | bytes 786440 | tf_op jit(solution)/shard_map/ppermute | solution.py:22
  224.8 13.0 %collective-permute-start.9 = (f32[2,128,256]{2,0,1:T(2,128)}, f32[2,128,256]{2,0,1:T(2,128)}, u32[]{:S(2)}, u32[]{:S(2)}) collective-permute-start(f32[2,128,256]{2,0,1:T(2,128)} %get-tuple-element.134), channel_id=1, source_target_pairs={{1,0},{2,1},{3,2},{4,3},{5,4},{6,5},{7,6},{9,8},{10,9},{11,10},{12... | collective-permute-start | bytes 786440 | tf_op jit(solution)/shard_map/ppermute | solution.py:24
  248.9 39.1 %collective-permute-start.10 = (f32[2,128,256]{2,0,1:T(2,128)}, f32[2,128,256]{2,0,1:T(2,128)}, u32[]{:S(2)}, u32[]{:S(2)}) collective-permute-start(f32[2,128,256]{2,0,1:T(2,128)} %get-tuple-element.129), channel_id=1, source_target_pairs={{0,1},{1,2},{2,3},{3,4},{4,5},{5,6},{6,7},{8,9},{9,10},{10,11},{11... | collective-permute-start | bytes 786440 | tf_op jit(solution)/shard_map/ppermute | solution.py:22
  253.6 34.5 %collective-permute-start.11 = (f32[2,128,256]{2,0,1:T(2,128)}, f32[2,128,256]{2,0,1:T(2,128)}, u32[]{:S(2)}, u32[]{:S(2)}) collective-permute-start(f32[2,128,256]{2,0,1:T(2,128)} %get-tuple-element.130), channel_id=1, source_target_pairs={{1,0},{2,1},{3,2},{4,3},{5,4},{6,5},{7,6},{9,8},{10,9},{11,10},{12... | collective-permute-start | bytes 786440 | tf_op jit(solution)/shard_map/ppermute | solution.py:24
  260.2 64.0 %collective-permute-start.13 = (f32[2,128,256]{2,0,1:T(2,128)}, f32[2,128,256]{2,0,1:T(2,128)}, u32[]{:S(2)}, u32[]{:S(2)}) collective-permute-start(f32[2,128,256]{2,0,1:T(2,128)} %copy.88), channel_id=1, source_target_pairs={{1,0},{2,1},{3,2},{4,3},{5,4},{6,5},{7,6},{9,8},{10,9},{11,10},{12... | collective-permute-start | bytes 786440 | tf_op jit(solution)/shard_map/ppermute | solution.py:24
  273.4 51.9 %collective-permute-start.12 = (f32[2,128,256]{2,0,1:T(2,128)}, f32[2,128,256]{2,0,1:T(2,128)S(1)}, u32[]{:S(2)}, u32[]{:S(2)}) collective-permute-start(f32[2,128,256]{2,0,1:T(2,128)} %copy.86), channel_id=1, source_target_pairs={{0,1},{1,2},{2,3},{3,4},{4,5},{5,6},{6,7},{8,9},{9,10},{10,11},{11... | collective-permute-start | bytes 786440 | tf_op jit(solution)/shard_map/ppermute | solution.py:22
  304.9 26.0 %copy-start.27 = (f32[8,128,256]{2,0,1:T(8,128)S(1)}, f32[8,128,256]{2,0,1:T(8,128)}, u32[]{:S(2)}) copy-start(f32[8,128,256]{2,0,1:T(8,128)} %copy-done.26) | copy-start | bytes 3145732
  304.9 26.0 %copy-start.29 = (f32[8,128,256]{2,0,1:T(8,128)S(1)}, f32[8,128,256]{2,0,1:T(8,128)}, u32[]{:S(2)}) copy-start(f32[8,128,256]{2,0,1:T(8,128)} %copy-done.28) | copy-start | bytes 3145732
  304.9 26.0 %copy-start.30 = (f32[8,128,256]{2,0,1:T(8,128)S(1)}, f32[8,128,256]{2,0,1:T(8,128)}, u32[]{:S(2)}) copy-start(f32[8,128,256]{2,0,1:T(8,128)} %get-tuple-element.85) | copy-start | bytes 3145732
  304.9 26.0 %copy-start.31 = (f32[8,128,256]{2,1,0:T(8,128)S(1)}, f32[8,128,256]{2,1,0:T(8,128)}, u32[]{:S(2)}) copy-start(f32[8,128,256]{2,1,0:T(8,128)} %reshape.387) | copy-start | bytes 3145732
  317.4 7.8 %collective-permute-start.14 = (f32[2,128,256]{2,0,1:T(2,128)S(1)}, f32[2,128,256]{2,0,1:T(2,128)S(1)}, u32[]{:S(2)}, u32[]{:S(2)}) collective-permute-start(f32[2,128,256]{2,0,1:T(2,128)S(1)} %get-tuple-element.127), channel_id=1, source_target_pairs={{0,1},{1,2},{2,3},{3,4},{4,5},{5,6},{6,7},{8,9},{9,10},{10,11},{11... | collective-permute-start | bytes 786440 | tf_op jit(solution)/shard_map/ppermute | solution.py:22
  321.9 8.9 %collective-permute-start.15 = (f32[2,128,256]{2,0,1:T(2,128)S(1)}, f32[2,128,256]{2,0,1:T(2,128)S(1)}, u32[]{:S(2)}, u32[]{:S(2)}) collective-permute-start(f32[2,128,256]{2,0,1:T(2,128)S(1)} %get-tuple-element.128), channel_id=1, source_target_pairs={{1,0},{2,1},{3,2},{4,3},{5,4},{6,5},{7,6},{9,8},{10,9},{11,10},{12... | collective-permute-start | bytes 786440 | tf_op jit(solution)/shard_map/ppermute | solution.py:24
  (51 other events, 483.8 us)
Sparse Core Ops, SparseCore 0:
  26.1 79.3 all-gather.1
  337.7 279.7 all-reduce.18
